TPU v7x, 128 devices: a whole 4x4x4 slice. The times are simulated.
128 devices in a mesh: walk: 2 (over core), orb: 64 (over z, y, x).
Axes of the slice: x: 4, y: 4, z: 4, core: 2. Of those that a mesh axis runs over, the one named last changes fastest.
Arguments:
- inverse: float32 [8, 2048, 2048], P('walk', 'orb'), may hold values from -6 to 6
- table: bfloat16 [512, 64, 2048], P(None, None, 'orb'), may hold values from -0.0119018555 to 0.0119018555
- old_rows: float32 [8, 16, 2048], P('walk', None, 'orb'), may hold values from -0.0046403883 to 0.0046403883
- spline_weights: bfloat16 [8, 16, 64], P('walk'), may hold values from 0.0099487305 to 0.099609375
- tile_index: int32 [8, 16], P('walk'), may hold values from 0 to 511
- electrons: int32 [8, 16], P('walk'), may hold values from 0 to 2047, as said below
- accepts: int32 [8, 16], P('walk'), may hold values 0 or 1
- offspring: int32 [8], P('walk'), may hold values from 0 to 3, as said below
Outputs:
- ratios: float32 [8, 16], P('walk')
- new_inverse: float32 [8, 2048, 2048], P('walk', 'orb')
Inputs may be any that keep to these rules, and one draw needn't show every extreme that they name: The 16 electrons of one walker are distinct. `offspring`: the counts of all walkers sum to 8.
All inputs are finite; a program needn't handle non-finite values. No bound on the sum of `accepts` on one device may be relied on, other than what follows from the above.
Results may differ from a plain program's by a relative error of at most 0.0003.
Values sent between devices are 32-bit elements; how exact they have to be, the bound alone decides.
A program may use at most 64 MiB of HBM per device.

v0:
```python
import jax
import jax.numpy as jnp
from jax import lax
from jax.sharding import PartitionSpec as P


def solve_small(matrix, rhs):
    count = matrix.shape[0]
    for index in range(count):
        pivot = matrix[index, index]
        mrow = matrix[index] / pivot
        brow = rhs[index] / pivot
        factor = matrix[:, index].at[index].set(0.0)
        matrix = matrix - factor[:, None] * mrow[None, :]
        matrix = matrix.at[index].set(mrow)
        rhs = rhs - factor[:, None] * brow[None, :]
        rhs = rhs.at[index].set(brow)
    return rhs


def move_ratios(cross, accept):
    count = cross.shape[0]
    order = jnp.arange(count)
    eye = jnp.eye(count, dtype=jnp.float32)

    def single(step):
        mask = accept * (order < step).astype(jnp.float32)
        system = eye + mask[:, None] * cross
        column = jnp.take(cross, step, axis=1)
        solved = solve_small(system, (mask * column)[:, None])[:, 0]
        rowm = jnp.take(cross, step, axis=0)
        return 1.0 + jnp.take(column, step) - jnp.sum(rowm * solved)

    return jax.vmap(single)(order)


def finish(inverse_one, projected, elec, accept):
    count = elec.shape[0]
    cross = projected[:, elec]
    system = jnp.eye(count, dtype=jnp.float32) + accept[:, None] * cross
    right = solve_small(system, accept[:, None] * projected)
    left = inverse_one[:, elec]
    return (inverse_one - jnp.dot(left, right, precision=lax.Precision.HIGHEST), cross)


def branch(matrices, source):
    walkers, rows_dev, columns = matrices.shape
    groups = lax.axis_size("walk")
    shaped = matrices.reshape(walkers, groups, rows_dev // groups, columns)
    blocks = lax.all_to_all(shaped, "walk", split_axis=1, concat_axis=0, tiled=True)
    picked = jnp.take(blocks, source, axis=0)
    back = lax.all_to_all(picked, "walk", split_axis=0, concat_axis=1, tiled=True)
    return back.reshape(walkers, rows_dev, columns)


def body(inverse, table, old_rows, spline_weights, tile_index, electrons, accepts, offspring):
    counts = lax.all_gather(offspring, "walk", axis=0, tiled=True)
    ends = jnp.cumsum(counts)
    slots = jnp.arange(counts.shape[0])
    source = jnp.sum((ends[None, :] <= slots[:, None]).astype(jnp.int32), axis=1)
    accept = accepts.astype(jnp.float32)
    picked = jnp.take(table, tile_index, axis=0)
    rows = jnp.einsum("wkc,wkco->wko", spline_weights, picked, preferred_element_type=jnp.float32)
    change = rows - old_rows
    term = jnp.einsum("wko,won->wkn", change, inverse, precision=lax.Precision.HIGHEST)
    projected = lax.psum(term, "orb")
    updated, cross = jax.vmap(finish)(inverse, projected, electrons, accept)
    ratios = jax.vmap(move_ratios)(cross, accept)
    new_inverse = branch(updated, source)
    return (ratios, new_inverse)


def solution(mesh):
    in_specs = (
        P("walk", "orb", None),
        P(None, None, "orb"),
        P("walk", None, "orb"),
        P("walk", None, None),
        P("walk", None),
        P("walk", None),
        P("walk", None),
        P("walk"),
    )
    out_specs = (P("walk", None), P("walk", "orb", None))
    return jax.shard_map(body, mesh=mesh, in_specs=in_specs, out_specs=out_specs, check_vma=False)
```

profile of v0, /device:TPU:1, one launch (start us, length us, event | category | flops | bytes accessed | tf_op | source)
XLA Modules:
  0.0 266.5 jit_solution(14458097727377886625)
XLA Ops:
  8.6 8.9 %copy.812 = bf16[512,64,32]{1,2,0:T(8,128)(2,1)} copy(bf16[512,64,32]{0,2,1:T(8,128)(2,1)} %param.197) | data formatting | bytes 4194304 | tf_op args[1]
  17.6 2.8 %gather_fusion = bf16[64,64,32]{1,2,0:T(8,128)(2,1)S(1)} fusion(bf16[512,64,32]{1,2,0:T(8,128)(2,1)} %copy.812, s32[1024]{0:T(1024)S(1)} %pad_clamp_fusion.2), kind=kCustom, calls=%fused_computation | custom fusion | bytes 524544 | tf_op jit(solution)/shard_map/jit(_take)/gather | solution.py:62
  20.9 1.4 fusion.8
  28.0 2.6 copy.853
  32.3 2.9 %all-reduce = s32[8]{0:T(128)S(1)} all-reduce(s32[8]{0:T(128)S(1)} %dynamic-update-slice.331), channel_id=1, replica_groups=mesh['walk'=2,'orb'=64] {'walk'}, use_global_device_ids=true, to_apply=%add | all-reduce | flops 8 | bytes 64
  35.6 1.5 gather_fusion.6
  37.2 113.8 %all-reduce.3.cloned.1.call-done = f32[4,16,2048]{2,1,0:T(8,128)} async-done(((f32[4,16,2048]{2,1,0:T(8,128)}), f32[4,16,2048]{2,1,0:T(8,128)}) %all-reduce.3.cloned.1.call-update) | async-done | bytes 524304 | tf_op jit(solution)/shard_map/psum | solution.py:66
  151.1 3.6 %copy.813 = f32[4,16,2048]{1,2,0:T(8,128)} copy(f32[4,16,2048]{2,1,0:T(8,128)} %all-reduce.3.cloned.1.call-done) | data formatting | bytes 1048576 | tf_op jit(solution)/shard_map/psum | solution.py:66
  154.6 1.5 gather_fusion.4
  157.5 0.8 select_bitcast_fusion.13
  158.7 1.2 scatter.400
  161.2 1.2 scatter.405
  163.6 1.2 scatter.410
  164.9 0.9 select_bitcast_fusion.10
  166.2 1.2 scatter.415
  167.4 0.8 select_bitcast_fusion.9
  168.7 1.2 scatter.420
  169.9 0.8 select_bitcast_fusion.8
  171.2 1.2 scatter.425
  172.5 0.8 select_bitcast_fusion.7
  173.8 1.2 scatter.430
  175.0 0.8 select_bitcast_fusion.6
  176.3 1.2 scatter.435
  177.5 0.9 select_bitcast_fusion.5
  178.9 1.2 scatter.440
  180.1 0.9 select_bitcast_fusion.4
  181.4 1.4 scatter.445
  182.9 0.9 select_bitcast_fusion.3
  184.2 1.2 scatter.450
  186.6 1.2 scatter.455
  187.9 0.9 select_bitcast_fusion.1
  189.2 1.2 scatter.460
  191.6 1.2 scatter.465
  199.7 1.0 convolution_subtract_fusion
  200.9 6.7 %all_to_all.33 = f32[4,2,16,2048]{3,2,0,1:T(8,128)S(1)} all-to-all(f32[4,2,16,2048]{3,2,0,1:T(8,128)S(1)} %copy.900), channel_id=1, replica_groups=mesh['walk'=2,'orb'=64] {'walk'}, dimensions={1} | all-to-all | bytes 2097152 | tf_op jit(solution)/shard_map/all_to_all | solution.py:50
  208.4 4.7 %all_to_all.34 = f32[8,1,16,2048]{3,2,1,0:T(8,128)S(1)} all-to-all(f32[8,1,16,2048]{3,2,1,0:T(8,128)S(1)} %fusion), channel_id=1, replica_groups=mesh['walk'=2,'orb'=64] {'walk'}, dimensions={0} | all-to-all | bytes 2097152 | tf_op jit(solution)/shard_map/all_to_all | solution.py:52
  213.1 1.1 copy.902
  217.7 0.8 multiply_subtract_fusion.59
  218.5 0.9 multiply_subtract_fusion.29
  220.6 0.8 multiply_subtract_fusion.58
  221.4 0.9 multiply_subtract_fusion.28
  223.5 0.8 multiply_subtract_fusion.57
  224.3 0.9 multiply_subtract_fusion.27
  226.4 0.8 multiply_subtract_fusion.56
  227.2 0.9 multiply_subtract_fusion.26
  229.3 0.8 multiply_subtract_fusion.55
  230.1 0.9 multiply_subtract_fusion.25
  232.2 0.8 multiply_subtract_fusion.54
  233.0 0.9 multiply_subtract_fusion.24
  235.2 0.8 multiply_subtract_fusion.53
  236.0 0.9 multiply_subtract_fusion.23
  238.1 0.8 multiply_subtract_fusion.52
  238.9 0.9 multiply_subtract_fusion.22
  241.0 0.8 multiply_subtract_fusion.51
  241.8 0.9 multiply_subtract_fusion.21
  243.9 0.8 multiply_subtract_fusion.50
  244.7 0.9 multiply_subtract_fusion.20
  246.8 0.8 multiply_subtract_fusion.49
  247.6 0.9 multiply_subtract_fusion.19
  250.5 0.9 multiply_subtract_fusion.18
  252.6 0.8 multiply_subtract_fusion.47
  253.4 0.9 multiply_subtract_fusion.17
  255.5 0.8 multiply_subtract_fusion.46
  256.3 0.9 multiply_subtract_fusion.16
  (333 shorter events, 49.9 us)
Async XLA Ops:
  7.2 13.2 %copy-start = (bf16[4,16,64]{2,1,0:T(8,128)(2,1)S(1)}, bf16[4,16,64]{2,1,0:T(8,128)(2,1)}, u32[]{:S(2)}) copy-start(bf16[4,16,64]{2,1,0:T(8,128)(2,1)} %param.199) | copy-start | bytes 24580
  7.2 143.9 %all-reduce.3.cloned.1.call-start = ((), (), s32[]{:S(2)}) async-start(), calls=%async_computation.2 | async-start | bytes 1048576 | tf_op jit(solution)/shard_map/psum | solution.py:66
  8.6 12.3 %copy-start.1 = (f32[4,32,2048]{2,1,0:T(8,128)S(1)}, f32[4,32,2048]{2,1,0:T(8,128)}, u32[]{:S(2)}) copy-start(f32[4,32,2048]{2,1,0:T(8,128)} %param.196) | copy-start | bytes 3145732
  8.6 12.3 %copy-start.3 = (f32[4,16,32]{2,1,0:T(8,128)S(1)}, f32[4,16,32]{2,1,0:T(8,128)}, u32[]{:S(2)}) copy-start(f32[4,16,32]{2,1,0:T(8,128)} %param.198) | copy-start | bytes 24580
  20.4 10.2 %copy-start.4 = (s32[4,16]{1,0:T(4,128)S(1)}, s32[4,16]{1,0:T(4,128)}, u32[]{:S(2)}) copy-start(s32[4,16]{1,0:T(4,128)} %param.201) | copy-start | bytes 772
  20.4 10.3 %copy-start.5 = (s32[4,16]{1,0:T(4,128)S(1)}, s32[4,16]{1,0:T(4,128)}, u32[]{:S(2)}) copy-start(s32[4,16]{1,0:T(4,128)} %param.202) | copy-start | bytes 772
  20.4 10.3 %copy-start.7 = (u32[128]{0:T(128)S(1)}, u32[128]{0:T(128)}, u32[]{:S(2)}) copy-start(u32[128]{0:T(128)} %constant.2468) | copy-start | bytes 1540
  20.5 11.5 %copy-start.6 = (s32[4]{0:T(128)S(1)}, s32[4]{0:T(128)}, u32[]{:S(2)}) copy-start(s32[4]{0:T(128)} %param.203) | copy-start | bytes 52
  151.1 42.1 %copy-start.2 = (f32[4,16,2048]{2,1,0:T(8,128)S(1)}, f32[4,16,2048]{2,1,0:T(8,128)}, u32[]{:S(2)}) copy-start(f32[4,16,2048]{2,1,0:T(8,128)} %all-reduce.3.cloned.1.call-done) | copy-start | bytes 1572868
Sparse Core Ops, SparseCore 0:
  22.5 128.4 all-reduce.2
where the time goes:
time: 269 us; the launch traced here: 266 us
  waiting for transfers between devices  114 us (42%)
  local copies, waits for them, and re-layouts  68.2 us (25%)
  other arithmetic  50.9 us (19%)
  between operations  16.2 us (6%)
  blocking collectives  14.3 us (5%)
  matrix products  2.93 us (1%)
    psum x1, waiting for transfers between devices, body(): projected = lax.psum(term, 'orb')  114 us
    scatter x15, local copies, waits for them, and re-layouts, solve_small(): matrix = matrix.at[index].set(mrow)  17.3 us
    sub x30, other arithmetic, solve_small(): matrix = matrix - factor[:, None] * mrow[None, :]  14.2 us
    unnamed x38, local copies, waits for them, and re-layouts  13.3 us
    sub x31, other arithmetic, solve_small(): rhs = rhs - factor[:, None] * brow[None, :]  12.7 us
    mul x30, other arithmetic, solve_small(): rhs = rhs - factor[:, None] * brow[None, :]  12.1 us
    scatter x32, local copies, waits for them, and re-layouts, solve_small(): factor = matrix[:, index].at[index].set(0.0)  9.69 us
    slice x16, local copies, waits for them, and re-layouts, solve_small(): factor = matrix[:, index].at[index].set(0.0)  8.56 us
  transfers between devices with their start and end apart: 1, of which 1 were waited for; matrix products, arithmetic and copies ran while one was open for 4% of the time, Pallas kernels for 0%

commit v1 on v0

--- a/solution.py
+++ b/solution.py
@@ -2,6 +2,12 @@
 import jax.numpy as jnp
 from jax import lax
 from jax.sharding import PartitionSpec as P
+
+
+def gather_and_add(block, axis):
+    shards = lax.all_gather(block, axis, axis=0, tiled=False)
+    total = shards.sum(axis=0)
+    return total
 
 
 def solve_small(matrix, rhs):
@@ -63,7 +69,7 @@
     rows = jnp.einsum("wkc,wkco->wko", spline_weights, picked, preferred_element_type=jnp.float32)
     change = rows - old_rows
     term = jnp.einsum("wko,won->wkn", change, inverse, precision=lax.Precision.HIGHEST)
-    projected = lax.psum(term, "orb")
+    projected = gather_and_add(term, "orb")
     updated, cross = jax.vmap(finish)(inverse, projected, electrons, accept)
     ratios = jax.vmap(move_ratios)(cross, accept)
     new_inverse = branch(updated, source)

time: 269 us -> 313 us (1.16)
  waiting for transfers between devices: 114 us -> 149 us
  other arithmetic: 50.9 us -> 62 us
    all_gather x0 -> x1, waiting for transfers between devices: none -> 149 us  [gather_and_add(): shards = lax.all_gather(block, axis, axis=0, tiled=False)]
    psum x1 -> x0, waiting for transfers between devices: 114 us -> none  [body(): projected = lax.psum(term, 'orb')]
    reduce_sum x0 -> x1, other arithmetic: none -> 11.7 us  [gather_and_add(): total = shards.sum(axis=0)]
    psum x1 -> x0, local copies, waits for them, and re-layouts: 3.56 us -> none  [body(): projected = lax.psum(term, 'orb')]
where the time goes in v1:
time: 313 us; the launch traced here: 310 us
  waiting for transfers between devices  149 us (48%)
  local copies, waits for them, and re-layouts  67.4 us (22%)
  other arithmetic  62 us (20%)
  between operations  16.2 us (5%)
  blocking collectives  12.4 us (4%)
    all_gather x1, waiting for transfers between devices, gather_and_add(): shards = lax.all_gather(block, axis, axis=0, tiled=False)  149 us
    scatter x15, local copies, waits for them, and re-layouts, solve_small(): matrix = matrix.at[index].set(mrow)  17.3 us
    sub x30, other arithmetic, solve_small(): matrix = matrix - factor[:, None] * mrow[None, :]  14.2 us
    unnamed x38, local copies, waits for them, and re-layouts  13.4 us
    sub x31, other arithmetic, solve_small(): rhs = rhs - factor[:, None] * brow[None, :]  12.7 us
    mul x30, other arithmetic, solve_small(): rhs = rhs - factor[:, None] * brow[None, :]  11.9 us
    reduce_sum x1, other arithmetic, gather_and_add(): total = shards.sum(axis=0)  11.7 us
    scatter x32, local copies, waits for them, and re-layouts, solve_small(): factor = matrix[:, index].at[index].set(0.0)  9.69 us
  transfers between devices with their start and end apart: 1, of which 1 were waited for; matrix products, arithmetic and copies ran while one was open for 4% of the time, Pallas kernels for 0%

profile of v1, /device:TPU:1, one launch (start us, length us, event | category | flops | bytes accessed | tf_op | source)
XLA Modules:
  0.0 310.4 jit_solution(13502864270399827231)
XLA Ops:
  8.6 8.9 %copy.812 = bf16[512,64,32]{1,2,0:T(8,128)(2,1)} copy(bf16[512,64,32]{0,2,1:T(8,128)(2,1)} %param.197) | data formatting | bytes 4194304 | tf_op args[1]
  17.6 2.8 gather_fusion
  20.9 1.4 fusion.8
  23.9 2.9 all-reduce
  26.8 2.7 copy.853
  30.0 1.5 gather_fusion.6
  37.1 149.4 %all-gather.3.cloned.1.call-done = f32[256,16,2048]{2,1,0:T(8,128)} async-done(((f32[4,16,2048]{2,1,0:T(8,128)}), f32[256,16,2048]{2,1,0:T(8,128)}) %all-gather.3.cloned.1.call-update) | async-done | bytes 33554448 | tf_op jit(solution)/shard_map/all_gather | solution.py:8
  186.5 11.7 %reduce_sum.29 = f32[4,16,2048]{2,1,0:T(8,128)S(1)} reduce(f32[64,4,16,2048]{3,2,1,0:T(8,128)} %bitcast.300, f32[]{:T(128)} %constant.2405.clone.1), dimensions={0}, to_apply=%region_0.0 | reduce | flops 8257536 | bytes 34078724 | tf_op jit(solution)/shard_map/reduce_sum | solution.py:9
  198.1 2.6 copy.813
  200.8 1.5 gather_fusion.4
  203.7 0.8 select_bitcast_fusion.13
  204.9 1.2 scatter.400
  206.2 0.9 select_bitcast_fusion.12
  207.5 1.2 scatter.405
  208.7 0.8 select_bitcast_fusion.11
  210.0 1.2 scatter.410
  211.3 0.9 select_bitcast_fusion.10
  212.6 1.2 scatter.415
  213.8 0.8 select_bitcast_fusion.9
  215.1 1.2 scatter.420
  217.6 1.2 scatter.425
  218.8 0.8 select_bitcast_fusion.7
  220.1 1.2 scatter.430
  222.5 1.2 scatter.435
  223.8 0.8 select_bitcast_fusion.5
  225.0 1.4 scatter.440
  227.6 1.2 scatter.445
  228.9 0.8 select_bitcast_fusion.3
  230.2 1.2 scatter.450
  232.6 1.2 scatter.455
  233.8 0.8 select_bitcast_fusion.1
  235.1 1.2 scatter.460
  237.6 1.2 scatter.465
  245.5 1.0 convolution_subtract_fusion
  246.6 4.9 %all_to_all.33 = f32[4,2,16,2048]{3,2,0,1:T(8,128)S(1)} all-to-all(f32[4,2,16,2048]{3,2,0,1:T(8,128)S(1)} %copy.900), channel_id=1, replica_groups=mesh['walk'=2,'orb'=64] {'walk'}, dimensions={1} | all-to-all | bytes 2097152 | tf_op jit(solution)/shard_map/all_to_all | solution.py:56
  252.3 4.7 %all_to_all.34 = f32[8,1,16,2048]{3,2,1,0:T(8,128)S(1)} all-to-all(f32[8,1,16,2048]{3,2,1,0:T(8,128)S(1)} %fusion), channel_id=1, replica_groups=mesh['walk'=2,'orb'=64] {'walk'}, dimensions={0} | all-to-all | bytes 2097152 | tf_op jit(solution)/shard_map/all_to_all | solution.py:58
  256.9 1.1 copy.902
  261.6 0.8 multiply_subtract_fusion.59
  262.4 0.9 multiply_subtract_fusion.29
  264.5 0.8 multiply_subtract_fusion.58
  265.3 0.9 multiply_subtract_fusion.28
  267.4 0.8 multiply_subtract_fusion.57
  268.2 0.9 multiply_subtract_fusion.27
  270.3 0.8 multiply_subtract_fusion.56
  271.1 0.9 multiply_subtract_fusion.26
  273.2 0.8 multiply_subtract_fusion.55
  274.0 0.9 multiply_subtract_fusion.25
  276.1 0.8 multiply_subtract_fusion.54
  276.9 0.9 multiply_subtract_fusion.24
  279.0 0.8 multiply_subtract_fusion.53
  279.8 0.9 multiply_subtract_fusion.23
  281.9 0.8 multiply_subtract_fusion.52
  282.7 0.9 multiply_subtract_fusion.22
  284.8 0.8 multiply_subtract_fusion.51
  285.6 0.9 multiply_subtract_fusion.21
  287.8 0.8 multiply_subtract_fusion.50
  288.6 0.9 multiply_subtract_fusion.20
  290.7 0.8 multiply_subtract_fusion.49
  291.5 0.9 multiply_subtract_fusion.19
  293.6 0.8 multiply_subtract_fusion.48
  294.4 0.9 multiply_subtract_fusion.18
  297.3 0.9 multiply_subtract_fusion.17
  299.4 0.8 multiply_subtract_fusion.46
  300.2 0.9 multiply_subtract_fusion.16
  (334 shorter events, 50.3 us)
Async XLA Ops:
  7.2 13.3 %copy-start = (bf16[4,16,64]{2,1,0:T(8,128)(2,1)S(1)}, bf16[4,16,64]{2,1,0:T(8,128)(2,1)}, u32[]{:S(2)}) copy-start(bf16[4,16,64]{2,1,0:T(8,128)(2,1)} %param.199) | copy-start | bytes 24580
  7.2 179.3 %all-gather.3.cloned.1.call-start = ((), (), s32[]{:S(2)}) async-start(), calls=%async_computation.2 | async-start | bytes 34078720 | tf_op jit(solution)/shard_map/all_gather | solution.py:8
  8.6 12.3 %copy-start.2 = (f32[4,32,2048]{2,1,0:T(8,128)S(1)}, f32[4,32,2048]{2,1,0:T(8,128)}, u32[]{:S(2)}) copy-start(f32[4,32,2048]{2,1,0:T(8,128)} %param.196) | copy-start | bytes 3145732
  8.6 12.3 %copy-start.3 = (f32[4,16,32]{2,1,0:T(8,128)S(1)}, f32[4,16,32]{2,1,0:T(8,128)}, u32[]{:S(2)}) copy-start(f32[4,16,32]{2,1,0:T(8,128)} %param.198) | copy-start | bytes 24580
  17.5 4.9 %copy-start.7 = (u32[128]{0:T(128)S(1)}, u32[128]{0:T(128)}, u32[]{:S(2)}) copy-start(u32[128]{0:T(128)} %constant.2468) | copy-start | bytes 1540
  17.5 6.2 %copy-start.6 = (s32[4]{0:T(128)S(1)}, s32[4]{0:T(128)}, u32[]{:S(2)}) copy-start(s32[4]{0:T(128)} %param.203) | copy-start | bytes 52
  20.4 9.1 %copy-start.4 = (s32[4,16]{1,0:T(4,128)S(1)}, s32[4,16]{1,0:T(4,128)}, u32[]{:S(2)}) copy-start(s32[4,16]{1,0:T(4,128)} %param.201) | copy-start | bytes 772
  20.4 9.2 %copy-start.5 = (s32[4,16]{1,0:T(4,128)S(1)}, s32[4,16]{1,0:T(4,128)}, u32[]{:S(2)}) copy-start(s32[4,16]{1,0:T(4,128)} %param.202) | copy-start | bytes 772
  285.6 17.9 %copy-start.1 = (bf16[4,16,64]{2,1,0:T(8,128)(2,1)S(1)}, bf16[4,16,64]{2,1,0:T(8,128)(2,1)}, u32[]{:S(2)}) copy-start(bf16[4,16,64]{2,1,0:T(8,128)(2,1)} %param.199) | copy-start | bytes 24580
Sparse Core Ops, SparseCore 0:
  22.5 163.9 all-gather.2
